TPU v7x, 128 devices: a whole 4x4x4 slice. The times are simulated.
128 devices in a mesh: row: 8 (over x_hi, y), col: 16 (over z, x_lo, core).
Axes of the slice: x: 4 (x_hi: 2, x_lo: 2; x = x_hi * 2 + x_lo), y: 4, z: 4, core: 2. Of those that a mesh axis runs over, the one named last changes fastest.
Arguments:
- fields: bfloat16 [128, 128, 1024], P('row', 'col'), may hold values from -6 to 6
- cotangent: bfloat16 [128, 128, 1024], P('row', 'col'), may hold values from -6 to 6
- query_weight: bfloat16 [1024, 1024], P(('row', 'col')), may hold values from -1 to 6
- key_weight: bfloat16 [1024, 1024], P(('row', 'col')), may hold values from -1 to 6
- value_weight: bfloat16 [1024, 1024], P(('row', 'col')), may hold values from -0.1875 to 0.1875
- output_weight: bfloat16 [1024, 1024], P(('row', 'col')), may hold values from -0.1875 to 0.1875
- expert_ids: int32 [8, 16, 128, 2], P('row', 'col'), may hold values from 0 to 31, all different within a row; in each aligned block of 128 rows (0 to 127, 128 to 255, ..., all dimensions but the last counted through in order) at most 10 rows name the same one
- gate_values: float32 [8, 16, 128, 2], P('row', 'col'), may hold values from 0.2 to 1
- gate_weight: bfloat16 [128, 1024, 1024], P(('row', 'col')), may hold values from -0.1875 to 0.1875
- up_weight: bfloat16 [128, 1024, 1024], P(('row', 'col')), may hold values from -0.1875 to 0.1875
- down_weight: bfloat16 [128, 1024, 1024], P(('row', 'col')), may hold values from -0.09375 to 0.09375
Outputs:
- field_grad: bfloat16 [128, 128, 1024], P('row', 'col')
- gate_grad: bfloat16 [128, 1024, 1024], P(('row', 'col'))
- up_grad: bfloat16 [128, 1024, 1024], P(('row', 'col'))
- down_grad: bfloat16 [128, 1024, 1024], P(('row', 'col'))
Inputs may be any that keep to these rules, and one draw needn't show every extreme that they name: `expert_ids`: the 2 entries of a cell differ; among one device's 128 cells no expert is named more than 10 times, a bound that some block reaches.
All inputs are finite; a program needn't handle non-finite values.
Results may differ from a plain program's by a relative error of at most 0.0095.
Values may be sent and summed in bfloat16 or wider, within the bound.
No kernel may reach another device: no remote copies, remote signals or barrier semaphores. Data moves between devices by JAX's collectives and lax.ppermute only.
A program may use at most 192 MiB of HBM per device.

v0:
```python
import math
import jax
import jax.numpy as jnp
from jax import lax
from jax.sharding import PartitionSpec as P

HEADS = 16
EXPERTS = 32
CAP = 10
EPS = 1e-06


def normalize(values):
    scale = lax.rsqrt(jnp.mean(values * values, axis=-1, keepdims=True) + EPS)
    return (values * scale, scale)


def norm_back(grads, normed, scale):
    return scale * (grads - normed * jnp.mean(grads * normed, axis=-1, keepdims=True))


def contract_rows(left, right):
    return lax.dot_general(
        left, right, (((0,), (0,)), ((), ())), preferred_element_type=jnp.float32
    )


def times_transposed(left, right):
    return lax.dot_general(
        left, right, (((1,), (1,)), ((), ())), preferred_element_type=jnp.float32
    )


def attention_forward(normed_half, query_weight, key_weight, value_weight, output_weight):
    latitudes, longitudes, features = normed_half.shape
    head_size = features // HEADS
    flat_rows = normed_half.reshape(latitudes * longitudes, features)

    def project(weight):
        result = jnp.dot(flat_rows, weight, preferred_element_type=jnp.float32)
        return result.astype(jnp.bfloat16).reshape(latitudes, longitudes, HEADS, head_size)

    queries = project(query_weight)
    key_rows = project(key_weight)
    value_rows = project(value_weight)
    factor = 1.0 / math.sqrt(head_size)
    scores = (
        jnp.einsum("bqhd,bkhd->bhqk", queries, key_rows, preferred_element_type=jnp.float32)
        * factor
    )
    attention = jax.nn.softmax(scores, axis=-1)
    attention_half = attention.astype(jnp.bfloat16)
    attended = jnp.einsum(
        "bhqk,bkhd->bqhd", attention_half, value_rows, preferred_element_type=jnp.float32
    ).astype(jnp.bfloat16)
    mixture = jnp.dot(
        attended.reshape(latitudes * longitudes, features),
        output_weight,
        preferred_element_type=jnp.float32,
    )
    return (mixture, (queries, key_rows, value_rows, attention, attention_half))


def attention_backward(block_half, stored, query_weight, key_weight, value_weight, output_weight):
    queries, key_rows, value_rows, attention, attention_half = stored
    latitudes, longitudes, head_count, head_size = queries.shape
    features = head_count * head_size
    factor = 1.0 / math.sqrt(head_size)
    out_grad = times_transposed(block_half.reshape(-1, features), output_weight)
    out_grad = out_grad.astype(jnp.bfloat16).reshape(latitudes, longitudes, head_count, head_size)
    mass_grad = jnp.einsum(
        "bqhd,bkhd->bhqk", out_grad, value_rows, preferred_element_type=jnp.float32
    )
    score_grad = (
        attention * (mass_grad - jnp.sum(attention * mass_grad, axis=-1, keepdims=True)) * factor
    )
    score_grad = score_grad.astype(jnp.bfloat16)
    query_grad = jnp.einsum(
        "bhqk,bkhd->bqhd", score_grad, key_rows, preferred_element_type=jnp.float32
    ).astype(jnp.bfloat16)
    key_grad = jnp.einsum(
        "bhqk,bqhd->bkhd", score_grad, queries, preferred_element_type=jnp.float32
    ).astype(jnp.bfloat16)
    value_grad = jnp.einsum(
        "bhqk,bqhd->bkhd", attention_half, out_grad, preferred_element_type=jnp.float32
    ).astype(jnp.bfloat16)
    total = times_transposed(query_grad.reshape(-1, features), query_weight)
    total = total + times_transposed(key_grad.reshape(-1, features), key_weight)
    return total + times_transposed(value_grad.reshape(-1, features), value_weight)


def expert_terms(inputs, mix_grad, gate_block, up_block, down_block):
    gate_pre = jnp.dot(inputs, gate_block, preferred_element_type=jnp.float32)
    up_pre = jnp.dot(inputs, up_block, preferred_element_type=jnp.float32)
    sigmoid_gate = jax.nn.sigmoid(gate_pre)
    swish_gate = gate_pre * sigmoid_gate
    hidden = (swish_gate * up_pre).astype(jnp.bfloat16)
    hidden_grad = times_transposed(mix_grad, down_block)
    gate_delta = (
        hidden_grad * up_pre * sigmoid_gate * (1.0 + gate_pre * (1.0 - sigmoid_gate))
    ).astype(jnp.bfloat16)
    up_delta = (hidden_grad * swish_gate).astype(jnp.bfloat16)
    down_term = contract_rows(hidden, mix_grad).astype(jnp.bfloat16)
    gate_term = contract_rows(inputs, gate_delta).astype(jnp.bfloat16)
    up_term = contract_rows(inputs, up_delta).astype(jnp.bfloat16)
    returned = times_transposed(gate_delta, gate_block) + times_transposed(up_delta, up_block)
    return (gate_term, up_term, down_term, returned)


def assignment_slots(chosen):
    onehot = (chosen[:, None] == jnp.arange(EXPERTS, dtype=jnp.int32)[None, :]).astype(jnp.int32)
    before = jnp.cumsum(onehot, axis=0) - onehot
    return jnp.sum(before * onehot, axis=1)


def body(
    fields,
    cotangent,
    query_weight,
    key_weight,
    value_weight,
    output_weight,
    expert_ids,
    gate_values,
    gate_weight,
    up_weight,
    down_weight,
):
    field_rows, cotangent_rows = (
        lax.all_to_all(fields, "col", split_axis=0, concat_axis=1, tiled=True),
        lax.all_to_all(cotangent, "col", split_axis=0, concat_axis=1, tiled=True),
    )
    query_all, key_all, value_all, output_all = (
        lax.all_gather(query_weight, ("row", "col"), axis=0, tiled=True),
        lax.all_gather(key_weight, ("row", "col"), axis=0, tiled=True),
        lax.all_gather(value_weight, ("row", "col"), axis=0, tiled=True),
        lax.all_gather(output_weight, ("row", "col"), axis=0, tiled=True),
    )
    latitudes, longitudes, features = field_rows.shape
    token_count = latitudes * longitudes
    top_count = expert_ids.shape[-1]
    fields_full = field_rows.astype(jnp.float32)
    normed_in, scale_in = normalize(fields_full)
    normed_in_half = normed_in.astype(jnp.bfloat16)
    mixture, stored = attention_forward(normed_in_half, query_all, key_all, value_all, output_all)
    mid_stream = (fields_full.reshape(token_count, features) + mixture).astype(jnp.bfloat16)
    normed_mid, scale_mid = normalize(mid_stream.astype(jnp.float32))
    normed_mid_half = normed_mid.astype(jnp.bfloat16)
    chosen = expert_ids.reshape(token_count * top_count)
    slot_index = assignment_slots(chosen)
    places = chosen * CAP + slot_index
    cotangent_full = cotangent_rows.reshape(token_count, features).astype(jnp.float32)
    weights = gate_values.reshape(token_count, top_count)
    mix_grad = (
        (weights[:, :, None] * cotangent_full[:, None, :])
        .astype(jnp.bfloat16)
        .reshape(token_count * top_count, features)
    )
    inputs = jnp.broadcast_to(
        normed_mid_half[:, None, :], (token_count, top_count, features)
    ).reshape(token_count * top_count, features)
    blank_buffer = jnp.zeros((EXPERTS * CAP, features), jnp.bfloat16)
    send_inputs = blank_buffer.at[places].set(inputs)
    send_grads = blank_buffer.at[places].set(mix_grad)
    row_devices = lax.axis_size("row")
    col_devices = lax.axis_size("col")
    all_devices = row_devices * col_devices
    slice_count = all_devices // EXPERTS

    def spread(buffer):
        widened = jnp.broadcast_to(
            buffer.reshape(EXPERTS, 1, CAP, features), (EXPERTS, slice_count, CAP, features)
        )
        return widened.reshape(all_devices, CAP, features)

    recv_inputs, recv_grads = (
        lax.all_to_all(
            spread(send_inputs), ("row", "col"), split_axis=0, concat_axis=0, tiled=True
        ),
        lax.all_to_all(spread(send_grads), ("row", "col"), split_axis=0, concat_axis=0, tiled=True),
    )
    row_count = all_devices * CAP
    gate_term, up_term, down_term, returned = expert_terms(
        recv_inputs.reshape(row_count, features),
        recv_grads.reshape(row_count, features),
        gate_weight[0],
        up_weight[0],
        down_weight[0],
    )
    coming_back = lax.all_to_all(
        returned.reshape(all_devices, CAP, features).astype(jnp.bfloat16),
        ("row", "col"),
        split_axis=0,
        concat_axis=0,
        tiled=True,
    ).astype(jnp.float32)
    summed = jnp.sum(coming_back.reshape(EXPERTS, slice_count, CAP, features), axis=1)
    gathered = summed.reshape(EXPERTS * CAP, features)[places]
    normed_grad = jnp.sum(gathered.reshape(token_count, top_count, features), axis=1)
    block_grad = cotangent_full + norm_back(normed_grad, normed_mid, scale_mid)
    block_half = block_grad.astype(jnp.bfloat16)
    branch_grad = attention_backward(
        block_half.reshape(latitudes, longitudes, features),
        stored,
        query_all,
        key_all,
        value_all,
        output_all,
    )
    field_total = block_grad + norm_back(
        branch_grad, normed_in.reshape(token_count, features), scale_in.reshape(token_count, 1)
    )
    field_half = field_total.astype(jnp.bfloat16).reshape(latitudes, longitudes, features)
    field_grad = lax.all_to_all(field_half, "col", split_axis=1, concat_axis=0, tiled=True)
    return (field_grad, gate_term[None], up_term[None], down_term[None])


def solution(mesh):
    in_specs = (
        P("row", "col", None),
        P("row", "col", None),
        P(("row", "col"), None),
        P(("row", "col"), None),
        P(("row", "col"), None),
        P(("row", "col"), None),
        P("row", "col", None, None),
        P("row", "col", None, None),
        P(("row", "col"), None, None),
        P(("row", "col"), None, None),
        P(("row", "col"), None, None),
    )
    out_specs = (
        P("row", "col", None),
        P(("row", "col"), None, None),
        P(("row", "col"), None, None),
        P(("row", "col"), None, None),
    )
    return jax.shard_map(body, mesh=mesh, in_specs=in_specs, out_specs=out_specs, check_vma=False)
```

profile of v0, /device:TPU:1, one launch (start us, length us, event | category | flops | bytes accessed | tf_op | source)
XLA Modules:
  0.0 1054.5 jit_solution(7280352464968909564)
XLA Ops:
  10.0 7.8 all-to-all-start
  20.7 4.3 all-to-all-done
  24.9 4.2 all-to-all-start.1
  39.8 9.7 all-to-all-start.2
  49.8 195.3 %all-gather.7.cloned.1.call-done = bf16[1024,1024]{1,0:T(8,128)(2,1)} async-done(((bf16[8,1024]{1,0:T(8,128)(2,1)}), bf16[1024,1024]{1,0:T(8,128)(2,1)}) %all-gather.7.cloned.1.call-update) | async-done | bytes 2097168 | tf_op jit(solution)/shard_map/all_gather | solution.py:134
  247.4 193.8 %all-gather.9.cloned.1.call-done = bf16[1024,1024]{1,0:T(8,128)(2,1)} async-done(((bf16[8,1024]{1,0:T(8,128)(2,1)}), bf16[1024,1024]{1,0:T(8,128)(2,1)}) %all-gather.9.cloned.1.call-update) | async-done | bytes 2097168 | tf_op jit(solution)/shard_map/all_gather | solution.py:135
  443.4 193.8 %all-gather.5.cloned.1.call-done = bf16[1024,1024]{1,0:T(8,128)(2,1)} async-done(((bf16[8,1024]{1,0:T(8,128)(2,1)}), bf16[1024,1024]{1,0:T(8,128)(2,1)}) %all-gather.5.cloned.1.call-update) | async-done | bytes 2097168 | tf_op jit(solution)/shard_map/all_gather | solution.py:136
  642.4 190.7 %all-gather.11.cloned.1.call-done = bf16[1024,1024]{1,0:T(8,128)(2,1)} async-done(((bf16[8,1024]{1,0:T(8,128)(2,1)}), bf16[1024,1024]{1,0:T(8,128)(2,1)}) %all-gather.11.cloned.1.call-update) | async-done | bytes 2097168 | tf_op jit(solution)/shard_map/all_gather | solution.py:137
  840.3 3.7 broadcast_in_dim.23
  844.0 8.2 all-to-all-start.3
  852.3 6.2 reshape.285
  858.5 46.5 %all-to-all-done.3 = bf16[128,10,1024]{2,1,0:T(8,128)(2,1)} async-done(((bf16[128,10,1024]{2,1,0:T(8,128)(2,1)}), bf16[128,10,1024]{2,1,0:T(8,128)(2,1)}, u32[]{:S(2)}, u32[]{:S(2)}) %all-to-all-start.3) | async-done | bytes 2621472 | tf_op jit(solution)/shard_map/all_to_all | solution.py:177
  905.0 6.1 reshape.288
  911.1 5.4 fusion.6
  920.2 5.9 multiply_convert_fusion.1
  929.1 4.4 add_convert_fusion
  933.4 6.0 convert_element_type.163
  939.4 6.7 all-to-all-start.4
  946.1 6.9 convert_bitcast_fusion.1
  953.1 8.6 convert_bitcast_fusion
  961.6 37.4 %all-to-all-done.4 = bf16[128,10,1024]{2,1,0:T(8,128)(2,1)} async-done(((bf16[128,10,1024]{2,1,0:T(8,128)(2,1)}), bf16[128,10,1024]{2,1,0:T(8,128)(2,1)}, u32[]{:S(2)}, u32[]{:S(2)}) %all-to-all-start.4) | async-done | bytes 2621472 | tf_op jit(solution)/shard_map/all_to_all | solution.py:190
  999.0 4.7 convert_reduce_fusion
  1035.2 4.3 all-to-all-start.5
  1039.5 6.9 convert_bitcast_fusion.2
  (130 shorter events, 72.3 us)
Async XLA Ops:
  7.2 912.3 %copy-start = (bf16[1,1024,1024]{2,1,0:T(8,128)(2,1)S(1)}, bf16[1,1024,1024]{2,1,0:T(8,128)(2,1)}, u32[]{:S(2)}) copy-start(bf16[1,1024,1024]{2,1,0:T(8,128)(2,1)} %param.21) | copy-start | bytes 6291460
  7.2 237.9 %all-gather.7.cloned.1.call-start = ((), (), s32[]{:S(2)}) async-start(), calls=%async_computation.7 | async-start | bytes 2113536 | tf_op jit(solution)/shard_map/all_gather | solution.py:134
  7.9 433.3 %all-gather.9.cloned.1.call-start = ((), (), s32[]{:S(2)}) async-start(), calls=%async_computation.8 | async-start | bytes 2113536 | tf_op jit(solution)/shard_map/all_gather | solution.py:135
  8.7 628.6 %all-gather.5.cloned.1.call-start = ((), (), s32[]{:S(2)}) async-start(), calls=%async_computation.6 | async-start | bytes 2113536 | tf_op jit(solution)/shard_map/all_gather | solution.py:136
  9.4 823.7 %all-gather.11.cloned.1.call-start = ((), (), s32[]{:S(2)}) async-start(), calls=%async_computation.9 | async-start | bytes 2113536 | tf_op jit(solution)/shard_map/all_gather | solution.py:137
  10.0 15.0 %all-to-all-start = ((bf16[16,8,1024]{2,1,0:T(8,128)(2,1)}), bf16[16,8,1024]{2,1,0:T(8,128)(2,1)S(1)}, u32[]{:S(2)}, u32[]{:S(2)}) async-start(bf16[16,8,1024]{2,1,0:T(8,128)(2,1)} %param.12), calls=%async_computation | async-start | bytes 524288 | tf_op jit(solution)/shard_map/all_to_all | solution.py:131
  24.9 5.2 copy-start.6
  24.9 12.4 %all-to-all-start.1 = ((bf16[16,8,1024]{2,1,0:T(8,128)(2,1)}), bf16[16,8,1024]{2,1,0:T(8,128)(2,1)S(1)}, u32[]{:S(2)}, u32[]{:S(2)}) async-start(bf16[16,8,1024]{2,1,0:T(8,128)(2,1)} %param.11), calls=%async_computation.1 | async-start | bytes 524288 | tf_op jit(solution)/shard_map/all_to_all | solution.py:130
  39.8 800.5 %all-to-all-start.2 = ((bf16[128,10,1024]{2,1,0:T(8,128)(2,1)}), bf16[128,10,1024]{2,1,0:T(8,128)(2,1)}, u32[]{:S(2)}, u32[]{:S(2)}) async-start(bf16[128,10,1024]{2,1,0:T(8,128)(2,1)} %bitcast.161), calls=%async_computation.2 | async-start | bytes 8388608 | tf_op jit(solution)/shard_map/all_to_all | solution.py:180
  247.4 393.6 %copy-start.14 = (bf16[128,1024]{0,1:T(8,128)(2,1)}, bf16[128,1024]{0,1:T(8,128)(2,1)S(1)}, u32[]{:S(2)}) copy-start(bf16[128,1024]{0,1:T(8,128)(2,1)S(1)} %copy.55) | copy-start | bytes 786436
  443.4 198.9 %copy-start.15 = (bf16[128,1024]{0,1:T(8,128)(2,1)}, bf16[128,1024]{0,1:T(8,128)(2,1)S(1)}, u32[]{:S(2)}) copy-start(bf16[128,1024]{0,1:T(8,128)(2,1)S(1)} %copy.56) | copy-start | bytes 786436
  844.0 60.9 %all-to-all-start.3 = ((bf16[128,10,1024]{2,1,0:T(8,128)(2,1)}), bf16[128,10,1024]{2,1,0:T(8,128)(2,1)}, u32[]{:S(2)}, u32[]{:S(2)}) async-start(bf16[128,10,1024]{2,1,0:T(8,128)(2,1)} %bitcast.162), calls=%async_computation.3 | async-start | bytes 8388608 | tf_op jit(solution)/shard_map/all_to_all | solution.py:177
  911.1 5.4 copy-start.8
  911.1 5.4 copy-start.20
  916.6 3.6 copy-start.9
  920.2 5.9 copy-start.24
  920.2 5.9 copy-start.19
  939.4 59.6 %all-to-all-start.4 = ((bf16[128,10,1024]{2,1,0:T(8,128)(2,1)}), bf16[128,10,1024]{2,1,0:T(8,128)(2,1)}, u32[]{:S(2)}, u32[]{:S(2)}) async-start(bf16[128,10,1024]{2,1,0:T(8,128)(2,1)} %convert_element_type.163), calls=%async_computation.4 | async-start | bytes 8388608 | tf_op jit(solution)/shard_map/all_to_all | solution.py:190
  946.1 6.9 copy-start.10
  1007.6 5.7 copy-start.5
  1013.1 3.8 copy-start.22
  1017.0 3.9 copy-start.16
  1035.2 11.4 %all-to-all-start.5 = ((bf16[16,2,4096]{2,1,0:T(2,128)(2,1)}), bf16[16,2,4096]{2,1,0:T(2,128)(2,1)S(1)}, u32[]{:S(2)}, u32[]{:S(2)}) async-start(bf16[16,2,4096]{2,1,0:T(2,128)(2,1)} %reshape.331), calls=%async_computation.5 | async-start | bytes 524288 | tf_op jit(solution)/shard_map/all_to_all | solution.py:214
  1039.5 8.2 copy-start.1
  (13 other events, 30.8 us)
Sparse Core Ops, SparseCore 0:
  9.7 235.3 all-gather.6
  246.8 194.2 all-gather.8
  442.9 194.2 all-gather.4
  638.8 194.2 all-gather.10
where the time goes:
time: 1060 us; the launch traced here: 1050 us
  waiting for transfers between devices  865 us (82%)
  matrix products  70.7 us (7%)
  local copies, waits for them, and re-layouts  49.5 us (5%)
  starting transfers between devices  41.1 us (4%)
  between operations  14.6 us (1%)
  other arithmetic  14.2 us (1%)
    all_gather x1, waiting for transfers between devices, body(): lax.all_gather(query_weight, ('row', 'col'), axis=0, tiled=True)  195 us
    all_gather x1, waiting for transfers between devices, body(): lax.all_gather(key_weight, ('row', 'col'), axis=0, tiled=True)  194 us
    all_gather x1, waiting for transfers between devices, body(): lax.all_gather(value_weight, ('row', 'col'), axis=0, tiled=True)  194 us
    all_gather x1, waiting for transfers between devices, body(): lax.all_gather(output_weight, ('row', 'col'), axis=0, tiled=True)  191 us
    all_to_all x1, waiting for transfers between devices, body(): lax.all_to_all(spread(send_inputs), ('row', 'col'), split_axis=0, concat_...  46.5 us
    all_to_all x1, waiting for transfers between devices, body(): lax.all_to_all(returned.reshape(all_devices, CAP, features).astype(jnp.bf...  37.4 us
    dot_general x3, matrix products, contract_rows(): lax.dot_general(left, right, (((0,), (0,)), ((), ())), preferred_element_...  22.5 us
  transfers between devices with their start and end apart: 10, of which 8 were waited for; matrix products, arithmetic and copies ran while one was open for 6% of the time, Pallas kernels for 0%

commit v1 on v0

--- a/solution.py
+++ b/solution.py
@@ -133,7 +133,12 @@
     query_all, key_all, value_all, output_all = (
         lax.all_gather(query_weight, ("row", "col"), axis=0, tiled=True),
         lax.all_gather(key_weight, ("row", "col"), axis=0, tiled=True),
-        lax.all_gather(value_weight, ("row", "col"), axis=0, tiled=True),
+        jnp.concatenate(
+            lax.all_to_all(
+                jnp.stack([value_weight] * lax.axis_size(("row", "col"))), ("row", "col"), 0, 0
+            ),
+            axis=0,
+        ),
         lax.all_gather(output_weight, ("row", "col"), axis=0, tiled=True),
     )
     latitudes, longitudes, features = field_rows.shape

time: 1060 us -> 883 us (0.83)
  waiting for transfers between devices: 865 us -> 671 us
  blocking collectives: 0 us -> 11.5 us
    all_gather x1 -> x0, waiting for transfers between devices: 194 us -> none  [body(): lax.all_gather(value_weight, ('row', 'col'), axis=0, tiled=True)]
    all_gather x1, waiting for transfers between devices: 194 us -> 171 us  [body(): lax.all_gather(key_weight, ('row', 'col'), axis=0, tiled=True)]
    all_to_all x1, waiting for transfers between devices: 4.25 us -> 21.8 us  [body(): lax.all_to_all(jnp.stack([value_weight] * lax.axis_size(('row', 'col'))),...]
    all_to_all x0 -> x1, blocking collectives: none -> 11.5 us  [body(): lax.all_to_all(cotangent, 'col', split_axis=0, concat_axis=1, tiled=True)]
  transfers between devices with their start and end apart: 10 -> 9, of which waited for: 8 -> 8; matrix products, arithmetic and copies ran while one was open for 6% -> 7% of each run, Pallas kernels for 0% -> 0%
where the time goes in v1:
time: 883 us; the launch traced here: 873 us
  waiting for transfers between devices  671 us (76%)
  matrix products  72.3 us (8%)
  local copies, waits for them, and re-layouts  49.5 us (6%)
  starting transfers between devices  40.4 us (5%)
  between operations  14.8 us (2%)
  other arithmetic  13.5 us (2%)
  blocking collectives  11.5 us (1%)
    all_gather x1, waiting for transfers between devices, body(): lax.all_gather(query_weight, ('row', 'col'), axis=0, tiled=True)  194 us
    all_gather x1, waiting for transfers between devices, body(): lax.all_gather(output_weight, ('row', 'col'), axis=0, tiled=True)  191 us
    all_gather x1, waiting for transfers between devices, body(): lax.all_gather(key_weight, ('row', 'col'), axis=0, tiled=True)  171 us
    all_to_all x1, waiting for transfers between devices, body(): lax.all_to_all(spread(send_inputs), ('row', 'col'), split_axis=0, concat_...  46.8 us
    all_to_all x1, waiting for transfers between devices, body(): lax.all_to_all(returned.reshape(all_devices, CAP, features).astype(jnp.bf...  37.4 us
    dot_general x3, matrix products, contract_rows(): lax.dot_general(left, right, (((0,), (0,)), ((), ())), preferred_element_...  22.5 us
    all_to_all x1, waiting for transfers between devices, body(): lax.all_to_all(jnp.stack([value_weight] * lax.axis_size(('row', 'col'))),...  21.8 us
    dot_general x7, matrix products, times_transposed(): lax.dot_general(left, right, (((1,), (1,)), ((), ())), preferred_element_...  21.7 us
  transfers between devices with their start and end apart: 9, of which 8 were waited for; matrix products, arithmetic and copies ran while one was open for 7% of the time, Pallas kernels for 0%

profile of v1, /device:TPU:1, one launch (start us, length us, event | category | flops | bytes accessed | tf_op | source)
XLA Modules:
  0.0 872.6 jit_solution(5125421836067008339)
XLA Ops:
  8.7 7.8 all-to-all-start.1
  17.2 6.5 all-to-all-done.1
  23.6 11.5 %all_to_all.50 = bf16[16,8,1024]{2,1,0:T(8,128)(2,1)S(1)} all-to-all(bf16[16,8,1024]{2,1,0:T(8,128)(2,1)} %param.12), channel_id=1, replica_groups=mesh['row'=8,'col'=16] {'col'}, dimensions={0} | all-to-all | bytes 524288 | tf_op jit(solution)/shard_map/all_to_all | solution.py:131
  37.4 8.2 all-to-all-start.2
  54.6 21.8 %all-to-all-done.2 = bf16[128,8,1024]{2,1,0:T(8,128)(2,1)} async-done(((bf16[128,8,1024]{2,1,0:T(8,128)(2,1)}), bf16[128,8,1024]{2,1,0:T(8,128)(2,1)}, u32[]{:S(2)}, u32[]{:S(2)}) %all-to-all-start.2) | async-done | bytes 2097184 | tf_op jit(solution)/shard_map/all_to_all | solution.py:137
  79.0 5.8 all-to-all-start.3
  87.3 171.3 %all-gather.6.cloned.1.call-done = bf16[1024,1024]{1,0:T(8,128)(2,1)} async-done(((bf16[8,1024]{1,0:T(8,128)(2,1)}), bf16[1024,1024]{1,0:T(8,128)(2,1)}) %all-gather.6.cloned.1.call-update) | async-done | bytes 2097168 | tf_op jit(solution)/shard_map/all_gather | solution.py:135
  260.9 193.8 %all-gather.4.cloned.1.call-done = bf16[1024,1024]{1,0:T(8,128)(2,1)} async-done(((bf16[8,1024]{1,0:T(8,128)(2,1)}), bf16[1024,1024]{1,0:T(8,128)(2,1)}) %all-gather.4.cloned.1.call-update) | async-done | bytes 2097168 | tf_op jit(solution)/shard_map/all_gather | solution.py:134
  459.8 190.9 %all-gather.8.cloned.1.call-done = bf16[1024,1024]{1,0:T(8,128)(2,1)} async-done(((bf16[8,1024]{1,0:T(8,128)(2,1)}), bf16[1024,1024]{1,0:T(8,128)(2,1)}) %all-gather.8.cloned.1.call-update) | async-done | bytes 2097168 | tf_op jit(solution)/shard_map/all_gather | solution.py:142
  661.7 7.5 all-to-all-start.4
  669.2 6.2 reshape.332
  675.4 46.8 %all-to-all-done.4 = bf16[128,10,1024]{2,1,0:T(8,128)(2,1)} async-done(((bf16[128,10,1024]{2,1,0:T(8,128)(2,1)}), bf16[128,10,1024]{2,1,0:T(8,128)(2,1)}, u32[]{:S(2)}, u32[]{:S(2)}) %all-to-all-start.4) | async-done | bytes 2621472 | tf_op jit(solution)/shard_map/all_to_all | solution.py:182
  722.2 6.1 reshape.335
  728.3 5.4 fusion.6
  737.4 5.9 multiply_convert_fusion.1
  746.2 4.4 add_convert_fusion
  750.6 5.9 convert_element_type.202
  756.6 6.7 all-to-all-start.5
  763.3 6.9 convert_bitcast_fusion.1
  770.3 8.6 convert_bitcast_fusion
  778.9 37.4 %all-to-all-done.5 = bf16[128,10,1024]{2,1,0:T(8,128)(2,1)} async-done(((bf16[128,10,1024]{2,1,0:T(8,128)(2,1)}), bf16[128,10,1024]{2,1,0:T(8,128)(2,1)}, u32[]{:S(2)}, u32[]{:S(2)}) %all-to-all-start.5) | async-done | bytes 2621472 | tf_op jit(solution)/shard_map/all_to_all | solution.py:195
  816.3 4.7 convert_reduce_fusion
  853.0 4.3 all-to-all-start.6
  857.4 6.9 convert_bitcast_fusion.2
  (129 shorter events, 76.4 us)
Async XLA Ops:
  7.2 729.5 %copy-start = (bf16[1,1024,1024]{2,1,0:T(8,128)(2,1)S(1)}, bf16[1,1024,1024]{2,1,0:T(8,128)(2,1)}, u32[]{:S(2)}) copy-start(bf16[1,1024,1024]{2,1,0:T(8,128)(2,1)} %param.21) | copy-start | bytes 6291460
  7.2 251.4 %all-gather.6.cloned.1.call-start = ((), (), s32[]{:S(2)}) async-start(), calls=%async_computation.8 | async-start | bytes 2113536 | tf_op jit(solution)/shard_map/all_gather | solution.py:135
  7.9 446.8 %all-gather.4.cloned.1.call-start = ((), (), s32[]{:S(2)}) async-start(), calls=%async_computation.7 | async-start | bytes 2113536 | tf_op jit(solution)/shard_map/all_gather | solution.py:134
  8.7 15.0 %all-to-all-start.1 = ((bf16[16,8,1024]{2,1,0:T(8,128)(2,1)}), bf16[16,8,1024]{2,1,0:T(8,128)(2,1)S(1)}, u32[]{:S(2)}, u32[]{:S(2)}) async-start(bf16[16,8,1024]{2,1,0:T(8,128)(2,1)} %param.11), calls=%async_computation.1 | async-start | bytes 524288 | tf_op jit(solution)/shard_map/all_to_all | solution.py:130
  16.4 634.3 %all-gather.8.cloned.1.call-start = ((), (), s32[]{:S(2)}) async-start(), calls=%async_computation.9 | async-start | bytes 2113536 | tf_op jit(solution)/shard_map/all_gather | solution.py:142
  35.1 12.4 %copy-start.4 = (bf16[16,8,1024]{2,1,0:T(8,128)(2,1)}, bf16[16,8,1024]{2,1,0:T(8,128)(2,1)S(1)}, u32[]{:S(2)}) copy-start(bf16[16,8,1024]{2,1,0:T(8,128)(2,1)S(1)} %all_to_all.50) | copy-start | bytes 786436
  37.4 8.2 copy-start.17
  37.4 9.7 %copy-start.18 = (f32[1,1,128,2]{2,3,1,0:T(2,128)S(1)}, f32[1,1,128,2]{2,3,1,0:T(2,128)}, u32[]{:S(2)}) copy-start(f32[1,1,128,2]{2,3,1,0:T(2,128)} %param.18) | copy-start | bytes 3076
  37.4 39.1 %all-to-all-start.2 = ((bf16[128,8,1024]{2,1,0:T(8,128)(2,1)}), bf16[128,8,1024]{2,1,0:T(8,128)(2,1)}, u32[]{:S(2)}, u32[]{:S(2)}) async-start(bf16[128,8,1024]{2,1,0:T(8,128)(2,1)} %stack.2), calls=%async_computation.2 | async-start | bytes 4194304 | tf_op jit(solution)/shard_map/all_to_all | solution.py:137
  79.0 578.9 %all-to-all-start.3 = ((bf16[128,10,1024]{2,1,0:T(8,128)(2,1)}), bf16[128,10,1024]{2,1,0:T(8,128)(2,1)}, u32[]{:S(2)}, u32[]{:S(2)}) async-start(bf16[128,10,1024]{2,1,0:T(8,128)(2,1)} %bitcast.181), calls=%async_computation.3 | async-start | bytes 8388608 | tf_op jit(solution)/shard_map/all_to_all | solution.py:185
  87.3 371.1 %copy-start.9 = (bf16[128,1024]{0,1:T(8,128)(2,1)}, bf16[128,1024]{0,1:T(8,128)(2,1)S(1)}, u32[]{:S(2)}) copy-start(bf16[128,1024]{0,1:T(8,128)(2,1)S(1)} %copy.54) | copy-start | bytes 786436
  260.9 198.9 %copy-start.11 = (bf16[128,1024]{0,1:T(8,128)(2,1)}, bf16[128,1024]{0,1:T(8,128)(2,1)S(1)}, u32[]{:S(2)}) copy-start(bf16[128,1024]{0,1:T(8,128)(2,1)S(1)} %copy.56) | copy-start | bytes 786436
  661.7 60.5 %all-to-all-start.4 = ((bf16[128,10,1024]{2,1,0:T(8,128)(2,1)}), bf16[128,10,1024]{2,1,0:T(8,128)(2,1)}, u32[]{:S(2)}, u32[]{:S(2)}) async-start(bf16[128,10,1024]{2,1,0:T(8,128)(2,1)} %bitcast.182), calls=%async_computation.4 | async-start | bytes 8388608 | tf_op jit(solution)/shard_map/all_to_all | solution.py:182
  728.3 5.4 copy-start.6
  728.3 5.4 copy-start.20
  733.7 3.6 copy-start.7
  737.4 5.9 copy-start.24
  737.4 5.9 copy-start.19
  756.6 59.7 %all-to-all-start.5 = ((bf16[128,10,1024]{2,1,0:T(8,128)(2,1)}), bf16[128,10,1024]{2,1,0:T(8,128)(2,1)}, u32[]{:S(2)}, u32[]{:S(2)}) async-start(bf16[128,10,1024]{2,1,0:T(8,128)(2,1)} %convert_element_type.202), calls=%async_computation.5 | async-start | bytes 8388608 | tf_op jit(solution)/shard_map/all_to_all | solution.py:195
  763.3 6.9 copy-start.8
  824.9 5.7 copy-start.3
  830.3 3.9 copy-start.22
  853.0 11.4 %all-to-all-start.6 = ((bf16[16,2,4096]{2,1,0:T(2,128)(2,1)}), bf16[16,2,4096]{2,1,0:T(2,128)(2,1)S(1)}, u32[]{:S(2)}, u32[]{:S(2)}) async-start(bf16[16,2,4096]{2,1,0:T(2,128)(2,1)} %reshape.379), calls=%async_computation.6 | async-start | bytes 524288 | tf_op jit(solution)/shard_map/all_to_all | solution.py:219
  857.4 8.2 copy-start.1
  (12 other events, 32.8 us)
Sparse Core Ops, SparseCore 0:
  9.7 248.8 all-gather.5
  260.3 194.2 all-gather.3
  456.4 194.2 all-gather.7
